TPU v7x, 32 devices: a whole 2x2x4 slice. The times are simulated.
32 devices in a mesh: groups: 2 (over x), gx: 4 (over y, core), gy: 4 (over z).
Axes of the slice: x: 2, y: 2, z: 4, core: 2. Of those that a mesh axis runs over, the one named last changes fastest.
Arguments:
- features: bfloat16 [8, 4, 4, 64, 256], P(('groups', 'gx'), 'gy'), parts along dimension 0, may hold values from -6 to 6
- neighbour_table: int32 [8, 4, 4, 27], P(('groups', 'gx'), 'gy'), parts along dimension 0, may hold values from 0 to 36, as said below
- kernel_weight: bfloat16 [27, 256, 256], replicated, may hold values from -0.078125 to 0.078125
- out_cotangent: bfloat16 [8, 4, 4, 64, 256], P(('groups', 'gx'), 'gy'), parts along dimension 0, may hold values from -6 to 6
Outputs:
- out_features: bfloat16 [8, 4, 4, 64, 256], P(('groups', 'gx'), 'gy'), parts along dimension 0
- grad_features: bfloat16 [8, 4, 4, 64, 256], P(('groups', 'gx'), 'gy'), parts along dimension 0
- grad_kernel: float32 [13824, 256], P(('groups', 'gx')), parts along dimension 0
There are 2 independent parts, one for each index of `groups`. A program takes and returns all parts, laid end to end along the dimension named above; an argument that names none is the same for every part. Nothing has to cross between parts.
Inputs may be any that keep to these rules, and one draw needn't show every extreme that they name: `neighbour_table`: within a tile the live slots come first; an empty slot has all 27 entries equal to 36; a live slot s has entry 16 + s at offset 13; adjacency is symmetric; some tile has all 4 slots live and the live counts differ much between tiles.
All inputs are finite; a program needn't handle non-finite values.
Results may differ from a plain program's by a relative error of at most 0.001.
Values may be sent and summed in bfloat16 or wider, within the bound.
A program may use at most 128 MiB of HBM per device.

v0:
```python
import functools

import jax
import jax.numpy as jnp
import numpy as np
from jax import lax
from jax.experimental import pallas as pl
from jax.experimental.pallas import tpu as pltpu
from jax.sharding import PartitionSpec as P

kernel_scale = 0.00390625
slots = 4
rows = 64
channels = 256
MESH = pl.DeviceIdType.MESH


def shift_matrix():
    out = np.zeros((9, 4, 4, 9, 4, 4), np.float32)
    for b in (-1, 0, 1):
        for c in (-1, 0, 1):
            for y in range(4):
                for z in range(4):
                    source = ((y + b) // 4 + 1) * 3 + (z + c) // 4 + 1
                    out[(b + 1) * 3 + c + 1, y, z, source, (y + b) % 4, (z + c) % 4] = 1
    return jnp.asarray(out.reshape(144, 144), jnp.bfloat16)


def ring_place(position, chips_y, chips_z):
    inner = chips_y * (chips_z - 1)
    y_in = position // (chips_z - 1)
    step = position % (chips_z - 1)
    z_in = jnp.where(y_in % 2 == 0, 1 + step, chips_z - 1 - step)
    on_edge = position >= inner
    y = jnp.where(on_edge, chips_y - 1 - (position - inner), y_in)
    z = jnp.where(on_edge, 0, z_in)
    return y, z


def ring_position(y, z, chips_y, chips_z):
    inside = y * (chips_z - 1) + jnp.where(y % 2 == 0, z - 1, chips_z - 1 - z)
    return jnp.where(z == 0, chips_y * (chips_z - 1) + chips_y - 1 - y, inside)


def gather_kernel(chips_y, chips_z, *refs):
    sources = refs[0:3]
    targets = refs[3:6]
    ring_send, ring_recv, pair_send, pair_recv = refs[6:]
    count = chips_y * chips_z
    half = count // 2
    gx = lax.axis_index("gx")
    z = lax.axis_index("gy")
    y = gx // 2
    core = gx % 2
    here = ring_position(y, z, chips_y, chips_z)

    def place(step):
        return ring_place((here + step + count) % count, chips_y, chips_z)

    def landing(stream, index):
        if stream == 0:
            return targets[0].at[index]
        return targets[(stream + 1) // 2].at[pl.ds(index * slots + (stream + 1) % 2 * 2, 2)]

    def origin(stream):
        if stream == 0:
            return sources[0].at[0]
        return sources[(stream + 1) // 2].at[pl.ds((stream + 1) % 2 * 2, 2)]

    def tile(step, which):
        ty, tz = place(step)
        return (ty * 2 + which) * chips_z + tz

    def device(step):
        ty, tz = place(step)
        return {"gx": ty * 2 + core, "gy": tz}

    partner = {"gx": y * 2 + 1 - core, "gy": z}
    near = (device(1), device(-1), partner)
    barrier = pltpu.get_barrier_semaphore()
    for peer in near:
        pl.semaphore_signal(barrier, inc=1, device_id=peer, device_id_type=MESH)

    def ring_copy(array, side, step):
        index = tile((1 - step) if side == 0 else (step - 1), core)
        src = origin(array) if step == 1 else landing(array, index)
        return pltpu.make_async_remote_copy(
            src_ref=src,
            dst_ref=landing(array, index),
            send_sem=ring_send.at[array, side, step - 1],
            recv_sem=ring_recv.at[array, side, step - 1],
            device_id=device(1) if side == 0 else device(-1),
            device_id_type=MESH,
        )

    def ring_wait(array, side, step):
        index = tile(-step if side == 0 else step, core)
        pltpu.make_async_remote_copy(
            src_ref=landing(array, index),
            dst_ref=landing(array, index),
            send_sem=ring_send.at[array, side, step - 1],
            recv_sem=ring_recv.at[array, side, step - 1],
            device_id=device(1),
            device_id_type=MESH,
        ).wait_recv()

    def pair_copy(array, step, which):
        number = step % count
        index = tile(step, which)
        src = origin(array) if step == 0 else landing(array, index)
        return pltpu.make_async_remote_copy(
            src_ref=src,
            dst_ref=landing(array, index),
            send_sem=pair_send.at[array, number],
            recv_sem=pair_recv.at[array, number],
            device_id=partner,
            device_id_type=MESH,
        )

    def reach(array, side):
        return half if (array % 2) == side else half - 1

    bricks = targets[1].shape[0] - 1
    mine = (gx * chips_z + z) * slots
    targets[0][gx * chips_z + z] = sources[0][0]
    for number in (1, 2):
        targets[number][pl.ds(mine, slots)] = sources[number][...]
        targets[number][bricks] = jnp.zeros((rows, channels), jnp.bfloat16)
    pl.semaphore_wait(barrier, 3)
    started = []
    for step in range(1, half + 2):
        for array in range(5):
            for side in (0, 1):
                if step - 1 > reach(array, side):
                    continue
                if step > 1:
                    ring_wait(array, side, step - 1)
                if step <= reach(array, side):
                    copy = ring_copy(array, side, step)
                    copy.start()
                    started.append(copy)
                if step > 1:
                    copy = pair_copy(array, (1 - step) if side == 0 else (step - 1), core)
                    copy.start()
                    started.append(copy)
            if step == 1:
                copy = pair_copy(array, 0, core)
                copy.start()
                started.append(copy)
    for array in range(5):
        for number in range(count):
            pair_copy(array, number, 1 - core).wait_recv()
    for copy in started:
        copy.wait_send()


def gather_tiles(table, cot, features, chips_y, chips_z):
    count = chips_y * chips_z
    tiles = 2 * count
    padded = (tiles * slots + 1, rows, channels)
    whole = pl.BlockSpec(memory_space=pltpu.VMEM)
    return pl.pallas_call(
        functools.partial(gather_kernel, chips_y, chips_z),
        out_shape=[
            jax.ShapeDtypeStruct((tiles, 1, 128), jnp.int32),
            pltpu.VMEM(padded, jnp.bfloat16),
            pltpu.VMEM(padded, jnp.bfloat16),
        ],
        in_specs=[whole] * 3,
        out_specs=[whole] * 3,
        scratch_shapes=[
            pltpu.SemaphoreType.DMA((5, 2, count // 2)),
            pltpu.SemaphoreType.DMA((5, 2, count // 2)),
            pltpu.SemaphoreType.DMA((5, count)),
            pltpu.SemaphoreType.DMA((5, count)),
        ],
        compiler_params=pltpu.CompilerParams(
            collective_id=0, has_side_effects=True, vmem_limit_bytes=12 * 2**20
        ),
        name="gather_tiles",
    )(table, cot, features)


def conv_kernel(bricks, part_rows, picked, gy_size, *refs):
    (table, shifts, cot, feat, weight_hbm, out_ref, grad_ref, term_hbm) = refs[:8]
    (weight, near, total, flat, order, sems) = refs[8:]
    gx = lax.axis_index("gx")
    gy = lax.axis_index("gy")
    weight_copy = pltpu.make_async_copy(weight_hbm, weight, sems.at[0])
    weight_copy.start()
    total[...] = jnp.zeros_like(total)

    def entry(brick, offset):
        return table[brick // slots, (brick % slots) * 32 + offset]

    def count_live(brick, found):
        @pl.when(entry(brick, 13) != bricks)
        def _():
            order[found] = brick

        return found + (entry(brick, 13) != bricks).astype(jnp.int32)

    live = lax.fori_loop(0, bricks, count_live, jnp.int32(0))
    for extra in range(slots):
        order[live + extra] = 0

    def surround(source, slot, brick, valid, both):
        names = []
        for offset in range(27):
            name = entry(brick, offset)
            names.append(name if valid is None else jnp.where(valid, name, bricks))
        def move(side, plane, x):
            stack = jnp.concatenate(
                [source[side[n], pl.ds(plane, 16), :] for n in range(9)], axis=0
            )
            moved = jnp.dot(shifts[...], stack, preferred_element_type=jnp.float32)
            near[:, slot, x] = moved.astype(jnp.bfloat16).reshape(9, 16, channels)

        for x in range(4):
            move(names[9:18], x * 16, x + 1)
        if both:
            move(names[:9], 48, 0)
            move(names[18:], 0, 5)
        else:
            outer = [jnp.where(behind, names[n], names[18 + n]) for n in range(9)]
            plane = pl.multiple_of(jnp.where(behind, 48, 0), 16)
            move(outer, plane, jnp.where(behind, 0, 5))

    def window(a, b, c):
        return near[(b + 1) * 3 + c + 1, :, pl.ds(1 + a, 4)].reshape(slots * rows, channels)

    first = (gx * part_rows) // channels
    last = jnp.minimum(first + picked - 1, 26)
    behind = last // 9 == 2

    def group(number, carry):
        names = []
        for slot in range(slots):
            place = number * slots + slot
            brick = order[place]
            valid = place < live
            surround(cot, slot, brick, valid, False)
            names.append(brick)
        block = jnp.concatenate([feat[name] for name in names], axis=0).T

        def one(n, inner):
            offset = jnp.minimum(first + n, 26)
            a = offset // 9 - 1
            b = (offset // 3) % 3 - 1
            c = offset % 3 - 1
            at = pl.multiple_of(n * channels, channels)
            total[pl.ds(at, channels), :] += jnp.dot(
                block, window(-a, -b, -c), preferred_element_type=jnp.float32
            )
            return inner

        return lax.fori_loop(0, picked, one, carry, unroll=True)

    lax.fori_loop(0, (live + slots - 1) // slots, group, 0)
    start = pl.multiple_of(gx * part_rows - first * channels, 8)
    span = pl.ds(start, part_rows)
    total[span, :] = total[span, :] * kernel_scale
    result = pltpu.make_async_copy(total.at[span], term_hbm, sems.at[1])
    result.start()
    weight_copy.wait()
    mine = (gx * gy_size + gy) * slots
    for sign, source, target in ((-1, cot, grad_ref), (1, feat, out_ref)):
        for slot in range(slots):
            surround(source, slot, mine + slot, None, True)
        for offset in range(27):
            a, b, c = offset // 9 - 1, (offset // 3) % 3 - 1, offset % 3 - 1
            dims = (((1,), (0 if sign == 1 else 1,)), ((), ()))
            product = lax.dot_general(
                window(sign * a, sign * b, sign * c),
                weight[offset],
                dims,
                preferred_element_type=jnp.float32,
            )
            if offset == 0:
                flat[...] = product
            elif offset < 26:
                flat[...] += product
            else:
                target[...] = (flat[...] + product).astype(jnp.bfloat16)
    result.wait()


def convolve(table_all, cot_all, feat_all, kernel_weight, part_rows, picked, gy_size):
    bricks = cot_all.shape[0] - 1
    own = (slots * rows, channels)
    whole = pl.BlockSpec(memory_space=pltpu.VMEM)
    far = pl.BlockSpec(memory_space=pltpu.HBM)
    return pl.pallas_call(
        functools.partial(conv_kernel, bricks, part_rows, picked, gy_size),
        out_shape=[
            jax.ShapeDtypeStruct(own, jnp.bfloat16),
            jax.ShapeDtypeStruct(own, jnp.bfloat16),
            jax.ShapeDtypeStruct((part_rows, channels), jnp.float32),
        ],
        in_specs=[pl.BlockSpec(memory_space=pltpu.SMEM), whole, whole, whole, far],
        out_specs=[whole, whole, far],
        scratch_shapes=[
            pltpu.VMEM(kernel_weight.shape, jnp.bfloat16),
            pltpu.VMEM((9, slots, 6, 16, channels), jnp.bfloat16),
            pltpu.VMEM((picked * channels, channels), jnp.float32),
            pltpu.VMEM(own, jnp.float32),
            pltpu.SMEM((bricks + slots,), jnp.int32),
            pltpu.SemaphoreType.DMA((2,)),
        ],
        compiler_params=pltpu.CompilerParams(vmem_limit_bytes=16 * 2**20),
        name="convolve",
    )(table_all, shift_matrix(), cot_all, feat_all, kernel_weight)


def body(gx_size, gy_size, features, neighbour_table, kernel_weight, out_cotangent):
    gx = lax.axis_index("gx")
    gy = lax.axis_index("gy")
    tiles = gx_size * gy_size
    bricks = tiles * slots
    table = neighbour_table[0, 0]
    block = table // slots
    owner = (gx + block // 3 - 1) * gy_size + gy + block % 3 - 1
    named = jnp.where(table == 9 * slots, bricks, owner * slots + table % slots)
    named = jnp.pad(named, ((0, 0), (0, 5))).reshape(1, 1, 128)
    flat = (slots, rows, channels)
    table_all, cot_all, feat_all = gather_tiles(
        named, out_cotangent.reshape(flat), features.reshape(flat), gx_size // 2, gy_size
    )
    part_rows = 27 * channels // gx_size
    picked = max(
        -(-((g + 1) * part_rows) // channels) - g * part_rows // channels for g in range(gx_size)
    )
    out, grad, term = convolve(
        table_all.reshape(tiles, 128),
        cot_all,
        feat_all,
        kernel_weight,
        part_rows,
        picked,
        gy_size,
    )
    return out.reshape(features.shape), grad.reshape(features.shape), term


def solution(mesh):
    in_specs = (
        P(("groups", "gx"), "gy", None, None, None),
        P(("groups", "gx"), "gy", None, None),
        P(),
        P(("groups", "gx"), "gy", None, None, None),
    )
    out_specs = (
        P(("groups", "gx"), "gy", None, None, None),
        P(("groups", "gx"), "gy", None, None, None),
        P(("groups", "gx"), None),
    )
    return jax.shard_map(
        functools.partial(body, mesh.shape["gx"], mesh.shape["gy"]),
        mesh=mesh,
        in_specs=in_specs,
        out_specs=out_specs,
        check_vma=False,
    )
```

profile of v0, /device:TPU:0, one launch (start us, length us, event | category | flops | bytes accessed | tf_op | source)
XLA Modules:
  0.0 52.2 jit_solution(10414691605597527606)
XLA Ops:
  0.6 0.7 %fusion.4 = s32[4,27]{1,0:T(4,128)S(1)} fusion(s32[1,1,4,27]{3,2,1,0:T(4,128)} %param.6, s32[]{:T(128)S(6)} %axis_index.25, s32[]{:T(128)S(6)} %axis_index.23), kind=kLoop, calls=%fused_computation.11 | loop fusion | flops 4428 | bytes 872 | tf_op jit(solution)/shard_map/jit(_where)/select_n | solution.py:323
  1.4 0.1 reshape.24.refs_0_
  1.4 0.0 copy-start.1
  1.4 0.9 %copy-done.1 = bf16[1,1,4,64,256]{4,3,2,1,0:T(8,128)(2,1)S(1)} copy-done((bf16[1,1,4,64,256]{4,3,2,1,0:T(8,128)(2,1)S(1)}, bf16[1,1,4,64,256]{4,3,2,1,0:T(8,128)(2,1)}, u32[]{:S(2)}) %copy-start.1) | copy-done | bytes 131096
  2.3 0.0 copy-start.2
  2.4 0.9 %copy-done.2 = bf16[1,1,4,64,256]{4,3,2,1,0:T(8,128)(2,1)S(1)} copy-done((bf16[1,1,4,64,256]{4,3,2,1,0:T(8,128)(2,1)S(1)}, bf16[1,1,4,64,256]{4,3,2,1,0:T(8,128)(2,1)}, u32[]{:S(2)}) %copy-start.2) | copy-done | bytes 131096
  3.3 28.7 %gather_tiles.1 = (s32[16,1,128]{2,1,0:T(1,128)S(1)}, bf16[65,64,256]{2,1,0:T(8,128)(2,1)S(1)}, bf16[65,64,256]{2,1,0:T(8,128)(2,1)S(1)}) custom-call(s32[1,1,128]{2,1,0:T(1,128)S(1)} %reshape.24.refs_0_, bf16[4,64,256]{2,1,0:T(8,128)(2,1)S(1)} %bitcast.26, bf16[4,64,256]{2,1,0:T(8,128)(2,1)S(1)} %bitcast.27), custom_call_target="tpu_custom_call" | custom-call | tf_op jit(solution)/shard_map/gather_tiles/pallas_call | solution.py:162
  31.9 0.0 copy-start
  32.0 2.0 %copy-done = bf16[27,256,256]{2,1,0:T(8,128)(2,1)S(1)} copy-done((bf16[27,256,256]{2,1,0:T(8,128)(2,1)S(1)}, bf16[27,256,256]{2,1,0:T(8,128)(2,1)}, u32[]{:S(2)}) %copy-start) | copy-done | bytes 3538968
  34.0 0.0 copy-start.3
  34.0 0.9 %copy-done.3 = bf16[144,144]{1,0:T(8,128)(2,1)S(1)} copy-done((bf16[144,144]{1,0:T(8,128)(2,1)S(1)}, bf16[144,144]{1,0:T(8,128)(2,1)}, u32[]{:S(2)}) %copy-start.3) | copy-done | bytes 41496
  34.8 17.3 %convolve.1 = (bf16[256,256]{1,0:T(8,128)(2,1)}, bf16[256,256]{1,0:T(8,128)(2,1)}, f32[1728,256]{1,0:T(8,128)}) custom-call(s32[16,128]{1,0:T(8,128)S(1)} %bitcast.28, bf16[144,144]{1,0:T(8,128)(2,1)S(1)} %copy-done.3, bf16[65,64,256]{2,1,0:T(8,128)(2,1)S(1)} %get-tuple-element.10.refs_2_, bf16[65,64,256]{2,1,0:T(8,128)(2,1)S(1)} %get-tuple-element.11.refs_3_, ...), custom_call_target="tpu_custom_call" | custom-call | tf_op jit(solution)/shard_map/convolve/pallas_call | solution.py:293
  (1 shorter events, 0.0 us)
Async XLA Ops:
  1.4 0.9 %copy-start.1 = (bf16[1,1,4,64,256]{4,3,2,1,0:T(8,128)(2,1)S(1)}, bf16[1,1,4,64,256]{4,3,2,1,0:T(8,128)(2,1)}, u32[]{:S(2)}) copy-start(bf16[1,1,4,64,256]{4,3,2,1,0:T(8,128)(2,1)} %param.8) | copy-start | bytes 393220
  2.3 0.9 %copy-start.2 = (bf16[1,1,4,64,256]{4,3,2,1,0:T(8,128)(2,1)S(1)}, bf16[1,1,4,64,256]{4,3,2,1,0:T(8,128)(2,1)}, u32[]{:S(2)}) copy-start(bf16[1,1,4,64,256]{4,3,2,1,0:T(8,128)(2,1)} %param.5) | copy-start | bytes 393220
  31.9 2.0 %copy-start = (bf16[27,256,256]{2,1,0:T(8,128)(2,1)S(1)}, bf16[27,256,256]{2,1,0:T(8,128)(2,1)}, u32[]{:S(2)}) copy-start(bf16[27,256,256]{2,1,0:T(8,128)(2,1)} %refs_4_.1) | copy-start | bytes 10616836
  34.0 0.9 %copy-start.3 = (bf16[144,144]{1,0:T(8,128)(2,1)S(1)}, bf16[144,144]{1,0:T(8,128)(2,1)}, u32[]{:S(2)}) copy-start(bf16[144,144]{1,0:T(8,128)(2,1)} %constant.57.clone.refs_1_) | copy-start | bytes 124420
where the time goes:
time: 52.6 us; the launch traced here: 52.2 us
  Pallas kernels  46 us (87%)
  local copies, waits for them, and re-layouts  4.78 us (9%)
  other arithmetic  0.71 us (1%)
  between operations  0.66 us (1%)
    pallas_call x1, Pallas kernels, gather_tiles(): pl.pallas_call(functools.partial(gather_kernel, chips_y, chips_z), out_sh...  28.7 us
    pallas_call x1, Pallas kernels, convolve(): pl.pallas_call(functools.partial(conv_kernel, bricks, part_rows, picked,...  17.3 us
    unnamed x8, local copies, waits for them, and re-layouts  4.69 us

commit v1 on v0

--- a/solution.py
+++ b/solution.py
@@ -45,7 +45,7 @@
 def gather_kernel(chips_y, chips_z, *refs):
     sources = refs[0:3]
     targets = refs[3:6]
-    ring_send, ring_recv, pair_send, pair_recv = refs[6:]
+    own_sem, ring_send, ring_recv, pair_send, pair_recv = refs[6:]
     count = chips_y * chips_z
     half = count // 2
     gx = lax.axis_index("gx")
@@ -123,8 +123,13 @@
     bricks = targets[1].shape[0] - 1
     mine = (gx * chips_z + z) * slots
     targets[0][gx * chips_z + z] = sources[0][0]
+    own = []
     for number in (1, 2):
-        targets[number][pl.ds(mine, slots)] = sources[number][...]
+        copy = pltpu.make_async_copy(
+            sources[number], targets[number].at[pl.ds(mine, slots)], own_sem.at[number - 1]
+        )
+        copy.start()
+        own.append(copy)
         targets[number][bricks] = jnp.zeros((rows, channels), jnp.bfloat16)
     pl.semaphore_wait(barrier, 3)
     started = []
@@ -150,8 +155,14 @@
     for array in range(5):
         for number in range(count):
             pair_copy(array, number, 1 - core).wait_recv()
+    for copy in own:
+        copy.wait()
     for copy in started:
         copy.wait_send()
+
+
+def keep_far(array):
+    return pltpu.with_memory_space_constraint(array, pltpu.HBM)
 
 
 def gather_tiles(table, cot, features, chips_y, chips_z):
@@ -166,9 +177,10 @@
             pltpu.VMEM(padded, jnp.bfloat16),
             pltpu.VMEM(padded, jnp.bfloat16),
         ],
-        in_specs=[whole] * 3,
+        in_specs=[whole, pl.BlockSpec(memory_space=pltpu.HBM), pl.BlockSpec(memory_space=pltpu.HBM)],
         out_specs=[whole] * 3,
         scratch_shapes=[
+            pltpu.SemaphoreType.DMA((2,)),
             pltpu.SemaphoreType.DMA((5, 2, count // 2)),
             pltpu.SemaphoreType.DMA((5, 2, count // 2)),
             pltpu.SemaphoreType.DMA((5, count)),
@@ -178,14 +190,16 @@
             collective_id=0, has_side_effects=True, vmem_limit_bytes=12 * 2**20
         ),
         name="gather_tiles",
-    )(table, cot, features)
+    )(table, keep_far(cot), keep_far(features))
 
 
 def conv_kernel(bricks, part_rows, picked, gy_size, *refs):
-    (table, shifts, cot, feat, weight_hbm, out_ref, grad_ref, term_hbm) = refs[:8]
-    (weight, near, total, flat, order, sems) = refs[8:]
+    (table, shift_hbm, cot, feat, weight_hbm, out_ref, grad_ref, term_hbm) = refs[:8]
+    (shifts, weight, near, total, flat, order, sems) = refs[8:]
     gx = lax.axis_index("gx")
     gy = lax.axis_index("gy")
+    shift_copy = pltpu.make_async_copy(shift_hbm, shifts, sems.at[2])
+    shift_copy.start()
     weight_copy = pltpu.make_async_copy(weight_hbm, weight, sems.at[0])
     weight_copy.start()
     total[...] = jnp.zeros_like(total)
@@ -229,6 +243,7 @@
     def window(a, b, c):
         return near[(b + 1) * 3 + c + 1, :, pl.ds(1 + a, 4)].reshape(slots * rows, channels)
 
+    shift_copy.wait()
     first = (gx * part_rows) // channels
     last = jnp.minimum(first + picked - 1, 26)
     behind = last // 9 == 2
@@ -297,19 +312,20 @@
             jax.ShapeDtypeStruct(own, jnp.bfloat16),
             jax.ShapeDtypeStruct((part_rows, channels), jnp.float32),
         ],
-        in_specs=[pl.BlockSpec(memory_space=pltpu.SMEM), whole, whole, whole, far],
+        in_specs=[pl.BlockSpec(memory_space=pltpu.SMEM), far, whole, whole, far],
         out_specs=[whole, whole, far],
         scratch_shapes=[
+            pltpu.VMEM((144, 144), jnp.bfloat16),
             pltpu.VMEM(kernel_weight.shape, jnp.bfloat16),
             pltpu.VMEM((9, slots, 6, 16, channels), jnp.bfloat16),
             pltpu.VMEM((picked * channels, channels), jnp.float32),
             pltpu.VMEM(own, jnp.float32),
             pltpu.SMEM((bricks + slots,), jnp.int32),
-            pltpu.SemaphoreType.DMA((2,)),
+            pltpu.SemaphoreType.DMA((3,)),
         ],
         compiler_params=pltpu.CompilerParams(vmem_limit_bytes=16 * 2**20),
         name="convolve",
-    )(table_all, shift_matrix(), cot_all, feat_all, kernel_weight)
+    )(table_all, keep_far(shift_matrix()), cot_all, feat_all, keep_far(kernel_weight))
 
 
 def body(gx_size, gy_size, features, neighbour_table, kernel_weight, out_cotangent):

time: 52.6 us -> 47.5 us (0.903)
  local copies, waits for them, and re-layouts: 4.78 us -> 0.09 us
    unnamed x8 -> x0, local copies, waits for them, and re-layouts: 4.69 us -> none
where the time goes in v1:
time: 47.5 us; the launch traced here: 47.3 us
  Pallas kernels  45.9 us (97%)
  other arithmetic  0.71 us (1%)
  between operations  0.65 us (1%)
    pallas_call x1, Pallas kernels, gather_tiles(): pl.pallas_call(functools.partial(gather_kernel, chips_y, chips_z), out_sh...  28.9 us
    pallas_call x1, Pallas kernels, convolve(): pl.pallas_call(functools.partial(conv_kernel, bricks, part_rows, picked,...  17 us

profile of v1, /device:TPU:0, one launch (start us, length us, event | category | flops | bytes accessed | tf_op | source)
XLA Modules:
  0.0 47.3 jit_solution(2959314580680406823)
XLA Ops:
  0.6 0.7 %fusion.4 = s32[4,27]{1,0:T(4,128)S(1)} fusion(s32[1,1,4,27]{3,2,1,0:T(4,128)} %param.6, s32[]{:T(128)S(6)} %axis_index.25, s32[]{:T(128)S(6)} %axis_index.23), kind=kLoop, calls=%fused_computation.11 | loop fusion | flops 4428 | bytes 872 | tf_op jit(solution)/shard_map/jit(_where)/select_n | solution.py:339
  1.4 0.1 reshape.24.refs_0_
  1.4 28.9 %gather_tiles.1 = (s32[16,1,128]{2,1,0:T(1,128)S(1)}, bf16[65,64,256]{2,1,0:T(8,128)(2,1)S(1)}, bf16[65,64,256]{2,1,0:T(8,128)(2,1)S(1)}) custom-call(s32[1,1,128]{2,1,0:T(1,128)S(1)} %reshape.24.refs_0_, bf16[4,64,256]{2,1,0:T(8,128)(2,1)} %bitcast.27, bf16[4,64,256]{2,1,0:T(8,128)(2,1)} %bitcast.28), custom_call_target="tpu_custom_call" | custom-call | tf_op jit(solution)/shard_map/gather_tiles/pallas_call | solution.py:173
  30.4 17.0 %convolve.1 = (bf16[256,256]{1,0:T(8,128)(2,1)}, bf16[256,256]{1,0:T(8,128)(2,1)}, f32[1728,256]{1,0:T(8,128)}) custom-call(s32[16,128]{1,0:T(8,128)S(1)} %bitcast.26, bf16[144,144]{1,0:T(8,128)(2,1)} %constant.57.clone.refs_1_, bf16[65,64,256]{2,1,0:T(8,128)(2,1)S(1)} %get-tuple-element.10.refs_2_, bf16[65,64,256]{2,1,0:T(8,128)(2,1)S(1)} %get-tuple-element.11.refs_3_, ...), custom_call_target="tpu_custom_call" | custom-call | tf_op jit(solution)/shard_map/convolve/pallas_call | solution.py:308
  (1 shorter events, 0.0 us)

commit v2 on v1

--- a/solution.py
+++ b/solution.py
@@ -44,8 +44,16 @@
 
 def gather_kernel(chips_y, chips_z, *refs):
     sources = refs[0:3]
-    targets = refs[3:6]
-    own_sem, ring_send, ring_recv, pair_send, pair_recv = refs[6:]
+    table, shift_hbm, weight_hbm = refs[3:6]
+    targets = refs[6:9]
+    grad_ref, shifts, weight, near, flat = refs[9:14]
+    own_sem, ring_send, ring_recv, pair_send, pair_recv = refs[14:]
+    loads = (
+        pltpu.make_async_copy(shift_hbm, shifts, own_sem.at[2]),
+        pltpu.make_async_copy(weight_hbm, weight, own_sem.at[3]),
+    )
+    for load in loads:
+        load.start()
     count = chips_y * chips_z
     half = count // 2
     gx = lax.axis_index("gx")
@@ -76,9 +84,9 @@
         return {"gx": ty * 2 + core, "gy": tz}
 
     partner = {"gx": y * 2 + 1 - core, "gy": z}
-    near = (device(1), device(-1), partner)
+    peers = (device(1), device(-1), partner)
     barrier = pltpu.get_barrier_semaphore()
-    for peer in near:
+    for peer in peers:
         pl.semaphore_signal(barrier, inc=1, device_id=peer, device_id_type=MESH)
 
     def ring_copy(array, side, step):
@@ -133,30 +141,71 @@
         targets[number][bricks] = jnp.zeros((rows, channels), jnp.bfloat16)
     pl.semaphore_wait(barrier, 3)
     started = []
-    for step in range(1, half + 2):
-        for array in range(5):
+    def launch(copy):
+        copy.start()
+        started.append(copy)
+
+    def advance(streams, step):
+        for stream in streams:
             for side in (0, 1):
-                if step - 1 > reach(array, side):
+                if step - 1 > reach(stream, side):
                     continue
                 if step > 1:
-                    ring_wait(array, side, step - 1)
-                if step <= reach(array, side):
-                    copy = ring_copy(array, side, step)
-                    copy.start()
-                    started.append(copy)
+                    ring_wait(stream, side, step - 1)
+                if step <= reach(stream, side):
+                    launch(ring_copy(stream, side, step))
                 if step > 1:
-                    copy = pair_copy(array, (1 - step) if side == 0 else (step - 1), core)
-                    copy.start()
-                    started.append(copy)
+                    launch(pair_copy(stream, (1 - step) if side == 0 else (step - 1), core))
             if step == 1:
-                copy = pair_copy(array, 0, core)
-                copy.start()
-                started.append(copy)
-    for array in range(5):
-        for number in range(count):
-            pair_copy(array, number, 1 - core).wait_recv()
-    for copy in own:
+                launch(pair_copy(stream, 0, core))
+
+    def settle(streams):
+        for stream in streams:
+            for number in range(count):
+                pair_copy(stream, number, 1 - core).wait_recv()
+
+    early, late = (0, 1, 2), (3, 4)
+    for step in range(1, half + 1):
+        advance(early, step)
+    advance(late, 1)
+    advance(early, half + 1)
+    settle(early)
+    for copy in own + list(loads):
         copy.wait()
+    cot = targets[1]
+
+    def own_slot(slot, carry):
+        names = [table[0, slot * 32 + offset] for offset in range(27)]
+        for x in range(6):
+            side = (x + 3) // 4
+            plane = (x + 3) % 4 * 16
+            stack = jnp.concatenate(
+                [cot[names[side * 9 + n], plane : plane + 16, :] for n in range(9)], axis=0
+            )
+            moved = jnp.dot(shifts[...], stack, preferred_element_type=jnp.float32)
+            near[:, slot, x] = moved.astype(jnp.bfloat16).reshape(9, 16, channels)
+        return carry
+
+    def pull(bc, carry):
+        for a in range(3):
+            seen = near[8 - bc, :, 2 - a : 6 - a].reshape(slots * rows, channels)
+            flat[...] += lax.dot_general(
+                seen,
+                weight[a * 9 + bc],
+                (((1,), (1,)), ((), ())),
+                preferred_element_type=jnp.float32,
+            )
+        return carry
+
+    flat[...] = jnp.zeros_like(flat)
+    lax.fori_loop(0, slots, own_slot, 0)
+    for step in range(2, half + 2):
+        advance(late, step)
+        low = 9 * (step - 2) // half
+        high = 9 * (step - 1) // half
+        lax.fori_loop(low, high, pull, 0)
+    grad_ref[...] = flat[...].astype(jnp.bfloat16)
+    settle(late)
     for copy in started:
         copy.wait_send()
 
@@ -165,9 +214,10 @@
     return pltpu.with_memory_space_constraint(array, pltpu.HBM)
 
 
-def gather_tiles(table, cot, features, chips_y, chips_z):
+def gather_tiles(table, cot, features, kernel_weight, chips_y, chips_z):
     count = chips_y * chips_z
     tiles = 2 * count
+    far = pl.BlockSpec(memory_space=pltpu.HBM)
     padded = (tiles * slots + 1, rows, channels)
     whole = pl.BlockSpec(memory_space=pltpu.VMEM)
     return pl.pallas_call(
@@ -176,11 +226,16 @@
             jax.ShapeDtypeStruct((tiles, 1, 128), jnp.int32),
             pltpu.VMEM(padded, jnp.bfloat16),
             pltpu.VMEM(padded, jnp.bfloat16),
+            pltpu.VMEM((slots * rows, channels), jnp.bfloat16),
         ],
-        in_specs=[whole, pl.BlockSpec(memory_space=pltpu.HBM), pl.BlockSpec(memory_space=pltpu.HBM)],
-        out_specs=[whole] * 3,
+        in_specs=[whole, far, far, pl.BlockSpec(memory_space=pltpu.SMEM), far, far],
+        out_specs=[whole] * 4,
         scratch_shapes=[
-            pltpu.SemaphoreType.DMA((2,)),
+            pltpu.VMEM((144, 144), jnp.bfloat16),
+            pltpu.VMEM(kernel_weight.shape, jnp.bfloat16),
+            pltpu.VMEM((9, slots, 6, 16, channels), jnp.bfloat16),
+            pltpu.VMEM((slots * rows, channels), jnp.float32),
+            pltpu.SemaphoreType.DMA((4,)),
             pltpu.SemaphoreType.DMA((5, 2, count // 2)),
             pltpu.SemaphoreType.DMA((5, 2, count // 2)),
             pltpu.SemaphoreType.DMA((5, count)),
@@ -190,12 +245,19 @@
             collective_id=0, has_side_effects=True, vmem_limit_bytes=12 * 2**20
         ),
         name="gather_tiles",
-    )(table, keep_far(cot), keep_far(features))
+    )(
+        table,
+        keep_far(cot),
+        keep_far(features),
+        table.reshape(1, 128),
+        keep_far(shift_matrix()),
+        keep_far(kernel_weight),
+    )
 
 
 def conv_kernel(bricks, part_rows, picked, gy_size, *refs):
-    (table, shift_hbm, cot, feat, weight_hbm, out_ref, grad_ref, term_hbm) = refs[:8]
-    (shifts, weight, near, total, flat, order, sems) = refs[8:]
+    (table, shift_hbm, cot, feat, weight_hbm, pulled, out_ref, grad_ref, term_hbm) = refs[:9]
+    (shifts, weight, near, total, flat, order, sems) = refs[9:]
     gx = lax.axis_index("gx")
     gy = lax.axis_index("gy")
     shift_copy = pltpu.make_async_copy(shift_hbm, shifts, sems.at[2])
@@ -279,7 +341,8 @@
     result.start()
     weight_copy.wait()
     mine = (gx * gy_size + gy) * slots
-    for sign, source, target in ((-1, cot, grad_ref), (1, feat, out_ref)):
+    grad_ref[...] = pulled[...]
+    for sign, source, target in ((1, feat, out_ref),):
         for slot in range(slots):
             surround(source, slot, mine + slot, None, True)
         for offset in range(27):
@@ -300,7 +363,7 @@
     result.wait()
 
 
-def convolve(table_all, cot_all, feat_all, kernel_weight, part_rows, picked, gy_size):
+def convolve(table_all, cot_all, feat_all, kernel_weight, pulled, part_rows, picked, gy_size):
     bricks = cot_all.shape[0] - 1
     own = (slots * rows, channels)
     whole = pl.BlockSpec(memory_space=pltpu.VMEM)
@@ -312,7 +375,7 @@
             jax.ShapeDtypeStruct(own, jnp.bfloat16),
             jax.ShapeDtypeStruct((part_rows, channels), jnp.float32),
         ],
-        in_specs=[pl.BlockSpec(memory_space=pltpu.SMEM), far, whole, whole, far],
+        in_specs=[pl.BlockSpec(memory_space=pltpu.SMEM), far, whole, whole, far, whole],
         out_specs=[whole, whole, far],
         scratch_shapes=[
             pltpu.VMEM((144, 144), jnp.bfloat16),
@@ -325,7 +388,7 @@
         ],
         compiler_params=pltpu.CompilerParams(vmem_limit_bytes=16 * 2**20),
         name="convolve",
-    )(table_all, keep_far(shift_matrix()), cot_all, feat_all, keep_far(kernel_weight))
+    )(table_all, keep_far(shift_matrix()), cot_all, feat_all, keep_far(kernel_weight), pulled)
 
 
 def body(gx_size, gy_size, features, neighbour_table, kernel_weight, out_cotangent):
@@ -339,8 +402,8 @@
     named = jnp.where(table == 9 * slots, bricks, owner * slots + table % slots)
     named = jnp.pad(named, ((0, 0), (0, 5))).reshape(1, 1, 128)
     flat = (slots, rows, channels)
-    table_all, cot_all, feat_all = gather_tiles(
-        named, out_cotangent.reshape(flat), features.reshape(flat), gx_size // 2, gy_size
+    table_all, cot_all, feat_all, pulled = gather_tiles(
+        named, out_cotangent.reshape(flat), features.reshape(flat), kernel_weight, gx_size // 2, gy_size
     )
     part_rows = 27 * channels // gx_size
     picked = max(
@@ -351,6 +414,7 @@
         cot_all,
         feat_all,
         kernel_weight,
+        pulled,
         part_rows,
         picked,
         gy_size,

time: 47.5 us -> 52.8 us (1.11)
  Pallas kernels: 45.9 us -> 51.1 us
    pallas_call x1, Pallas kernels: 28.9 us -> 36.5 us  [gather_tiles(): pl.pallas_call(functools.partial(gather_kernel, chips_y, chips_z), out_sh...]
    pallas_call x1, Pallas kernels: 17 us -> 14.6 us  [convolve(): pl.pallas_call(functools.partial(conv_kernel, bricks, part_rows, picked,...]
where the time goes in v2:
time: 52.8 us; the launch traced here: 52.6 us
  Pallas kernels  51.1 us (97%)
  other arithmetic  0.71 us (1%)
  between operations  0.65 us (1%)
    pallas_call x1, Pallas kernels, gather_tiles(): pl.pallas_call(functools.partial(gather_kernel, chips_y, chips_z), out_sh...  36.5 us
    pallas_call x1, Pallas kernels, convolve(): pl.pallas_call(functools.partial(conv_kernel, bricks, part_rows, picked,...  14.6 us

profile of v2, /device:TPU:0, one launch (start us, length us, event | category | flops | bytes accessed | tf_op | source)
XLA Modules:
  0.0 52.6 jit_solution(15609147409338740202)
XLA Ops:
  0.6 0.7 %fusion.4 = s32[4,27]{1,0:T(4,128)S(1)} fusion(s32[1,1,4,27]{3,2,1,0:T(4,128)} %param.7, s32[]{:T(128)S(6)} %axis_index.25, s32[]{:T(128)S(6)} %axis_index.23), kind=kLoop, calls=%fused_computation.11 | loop fusion | flops 4428 | bytes 872 | tf_op jit(solution)/shard_map/jit(_where)/select_n | solution.py:402
  1.4 0.1 reshape_reshape.3.refs_3_
  1.4 0.1 reshape.24.refs_0_
  1.5 36.5 %gather_tiles.1 = (s32[16,1,128]{2,1,0:T(1,128)S(1)}, bf16[65,64,256]{2,1,0:T(8,128)(2,1)S(1)}, bf16[65,64,256]{2,1,0:T(8,128)(2,1)S(1)}, bf16[256,256]{1,0:T(8,128)(2,1)S(1)}) custom-call(s32[1,1,128]{2,1,0:T(1,128)S(1)} %reshape.24.refs_0_, bf16[4,64,256]{2,1,0:T(8,128)(2,1)} %bitcast.27, bf16[4,64,256]{2,1,0:T(8,128)(2,1)} %bitcast.28, ...), custom_call_target="tpu_custom_call" | custom-call | tf_op jit(solution)/shard_map/gather_tiles/pallas_call | solution.py:223
  38.1 14.6 %convolve.1 = (bf16[256,256]{1,0:T(8,128)(2,1)}, bf16[256,256]{1,0:T(8,128)(2,1)}, f32[1728,256]{1,0:T(8,128)}) custom-call(s32[16,128]{1,0:T(8,128)S(1)} %bitcast.26, bf16[144,144]{1,0:T(8,128)(2,1)} %constant.57.clone.refs_4_.refs_1_, bf16[65,64,256]{2,1,0:T(8,128)(2,1)S(1)} %get-tuple-element.11.refs_2_, ...), custom_call_target="tpu_custom_call" | custom-call | tf_op jit(solution)/shard_map/convolve/pallas_call | solution.py:371
  (1 shorter events, 0.0 us)
